TPU v7x, 512 devices: a whole 4x8x8 slice. The times are simulated.
512 devices in a mesh: ty: 16 (over x_lo, z), tx: 32 (over y, x_hi, core).
Axes of the slice: x: 4 (x_hi: 2, x_lo: 2; x = x_hi * 2 + x_lo), y: 8, z: 8, core: 2. Of those that a mesh axis runs over, the one named last changes fastest.
Arguments:
- observed: float32 [6, 2048, 8192], P(None, 'ty', 'tx'), may hold values from -6 to 6
- inverse_variance: float32 [6, 2048, 8192], P(None, 'ty', 'tx'), may hold values from 0.5 to 4
- sed: float32 [16, 32, 6], P('ty', 'tx'), may hold values from 0.2 to 2
- morph: float32 [16, 32, 128, 128], P('ty', 'tx'), may hold values from 0.02 to 1
- foot_block: int32 [16, 32], P('ty', 'tx'), may hold values from 0 to 63, as said below
- gamma: float32 [16, 32], P('ty', 'tx'), may hold values from 0.3 to 1.5
- row_kernel: float32 [6, 41], replicated, may hold values from -1 to 1
- col_kernel: float32 [6, 41], replicated, may hold values from -1 to 1
Outputs:
- residual: float32 [6, 2048, 8192], P(None, 'ty', 'tx')
- new_morph: float32 [16, 32, 128, 128], P('ty', 'tx')
- new_sed: float32 [16, 32, 6], P('ty', 'tx')
Inputs may be any that keep to these rules, and one draw needn't show every extreme that they name: A source's footprint lies in its own tile row, at box column foot_block counted over the whole row; in every tile row at most 2 sources lie in one tile of 2 box columns, and some tile holds exactly 2.
All inputs are finite; a program needn't handle non-finite values.
Results may differ from a plain program's by a relative error of at most 0.0003.
Values sent between devices are 32-bit elements; how exact they have to be, the bound alone decides.
A program may use at most 64 MiB of HBM per device.

v0:
```python
import jax
import jax.numpy as jnp
from jax import lax
from jax.sharding import PartitionSpec as P

HIGHEST_PRECISION = lax.Precision.HIGHEST


def with_halo(value, sides, width):
    for axis, dim in sides:
        devices, length = (lax.axis_size(axis), value.shape[dim])
        up = [(i, (i + 1) % devices) for i in range(devices - 1)]
        down = [(j, i) for i, j in up]
        last = lax.slice_in_dim(value, length - width, length, axis=dim)
        leading = lax.slice_in_dim(value, 0, width, axis=dim)
        before = lax.ppermute(last, axis, up)
        after = lax.ppermute(leading, axis, down)
        value = jnp.concatenate([before, value, after], axis=dim)
    return value


def taps_matrix(kernel, length):
    taps_count = kernel.shape[1]
    span = length + taps_count - 1
    offset = (
        jnp.arange(span, dtype=jnp.int32)[:, None] - jnp.arange(length, dtype=jnp.int32)[None, :]
    )
    select = (offset[None] == jnp.arange(taps_count, dtype=jnp.int32)[:, None, None]).astype(
        jnp.float32
    )
    return jnp.einsum("bt,tqc->bqc", kernel, select, precision=HIGHEST_PRECISION)


def apply_columns(padded, matrix, per_tile, box_size):
    window = matrix.shape[1]
    windows = jnp.stack(
        [padded[:, :, block * box_size : block * box_size + window] for block in range(per_tile)],
        axis=2,
    )
    mixed = jnp.einsum("brjq,bqc->brjc", windows, matrix, precision=HIGHEST_PRECISION)
    return mixed.reshape(padded.shape[0], padded.shape[1], per_tile * box_size)


def body(observed, inverse_variance, sed, morph, foot_block, gamma, row_kernel, col_kernel):
    band_count, tile_rows, tile_cols = observed.shape
    box_size = morph.shape[2]
    per_tile = tile_cols // box_size
    rim_width = (row_kernel.shape[1] - 1) // 2
    all_sed, all_morph, all_foot = (
        lax.all_gather(sed, "tx", axis=1, tiled=True),
        lax.all_gather(morph, "tx", axis=1, tiled=True),
        lax.all_gather(foot_block, "tx", axis=1, tiled=True),
    )
    all_sed = all_sed[0]
    all_morph = all_morph[0]
    all_foot = all_foot[0]
    tile_index = lax.axis_index("tx")
    first_block = tile_index * per_tile
    placed = (
        all_foot[:, None] == first_block + jnp.arange(per_tile, dtype=jnp.int32)[None, :]
    ).astype(jnp.float32)
    weighted = placed[:, None, :] * all_sed[:, :, None]
    model = jnp.einsum("kbj,krc->brjc", weighted, all_morph, precision=HIGHEST_PRECISION).reshape(
        band_count, tile_rows, tile_cols
    )
    flip_rows = taps_matrix(row_kernel[:, ::-1], tile_rows)
    flip_cols = taps_matrix(col_kernel[:, ::-1], box_size)
    wide_model = with_halo(model, (("tx", 2),), rim_width)
    blurred = apply_columns(wide_model, flip_cols, per_tile, box_size)
    tall_blurred = with_halo(blurred, (("ty", 1),), rim_width)
    predicted = jnp.einsum("bqw,bqr->brw", tall_blurred, flip_rows, precision=HIGHEST_PRECISION)
    residual = inverse_variance * (observed - predicted)
    corr_rows = taps_matrix(row_kernel, tile_rows)
    corr_cols = taps_matrix(col_kernel, box_size)
    tall_resid = with_halo(residual, (("ty", 1),), rim_width)
    backrows = jnp.einsum("bqw,bqr->brw", tall_resid, corr_rows, precision=HIGHEST_PRECISION)
    wide_back = with_halo(backrows, (("tx", 2),), rim_width)
    gradient = apply_columns(wide_back, corr_cols, per_tile, box_size)
    grid = gradient.reshape(band_count, tile_rows, per_tile, box_size)
    morph_terms = jnp.einsum("kbj,brjc->krc", weighted, grid, precision=HIGHEST_PRECISION)
    raw_terms = jnp.einsum("krc,brjc->kbj", all_morph, grid, precision=HIGHEST_PRECISION)
    sed_terms = jnp.sum(raw_terms * placed[:, None, :], axis=2)
    morph_grad, sed_grad = (
        lax.psum_scatter(morph_terms, "tx", scatter_dimension=0, tiled=True),
        lax.psum_scatter(sed_terms, "tx", scatter_dimension=0, tiled=True),
    )
    own_sed = sed[0]
    own_morph = morph[0]
    own_gamma = gamma[0]
    step_morph = own_gamma / jnp.sum(own_sed * own_sed, axis=1)
    new_morph = jnp.maximum(own_morph + step_morph[:, None, None] * morph_grad, 0.0)
    step_sed = own_gamma / jnp.sqrt(jnp.sum(own_morph * own_morph, axis=(1, 2)))
    new_sed = jnp.maximum(own_sed + step_sed[:, None] * sed_grad, 0.0)
    return (residual, new_morph[None], new_sed[None])


def solution(mesh):
    in_specs = (
        P(None, "ty", "tx"),
        P(None, "ty", "tx"),
        P("ty", "tx", None),
        P("ty", "tx", None, None),
        P("ty", "tx"),
        P("ty", "tx"),
        P(),
        P(),
    )
    out_specs = (P(None, "ty", "tx"), P("ty", "tx", None, None), P("ty", "tx", None))
    return jax.shard_map(body, mesh=mesh, in_specs=in_specs, out_specs=out_specs, check_vma=False)
```

profile of v0, /device:TPU:96, one launch (start us, length us, event | category | flops | bytes accessed | tf_op | source)
XLA Modules:
  0.0 315.2 jit_solution(1384068626255635407)
XLA Ops:
  7.2 0.0 all-gather.2.cloned.1.call-start
  7.2 0.7 all-gather.2.cloned.1.call-update
  7.9 0.0 reduce-scatter.2.cloned.1.call-start
  8.6 0.8 rev.7
  9.4 39.6 %all_gather.10 = f32[1,32,6]{2,0,1:T(1,128)S(1)} all-gather(f32[1,1,6]{2,0,1:T(1,128)} %bitcast.108), channel_id=1, replica_groups=mesh['ty'=16,'tx'=32] {'tx'}, dimensions={1}, use_global_device_ids=true | all-gather | bytes 792 | tf_op jit(solution)/shard_map/all_gather | solution.py:50
  48.9 0.1 copy.32
  49.0 1.4 fusion.78
  50.4 0.7 bitcast_dynamic-update-slice_fusion
  51.1 13.8 %all-reduce = s32[32]{0:T(128)S(1)} all-reduce(s32[32]{0:T(128)S(1)} %bitcast_dynamic-update-slice_fusion), channel_id=1, replica_groups=mesh['ty'=16,'tx'=32] {'tx'}, use_global_device_ids=true, to_apply=%add | all-reduce | flops 32 | bytes 256
  64.9 0.1 compare_convert_fusion
  65.0 32.4 %all-gather.2.cloned.1.call-done = f32[1,32,128,128]{3,2,0,1:T(8,128)} async-done(((f32[1,1,128,128]{3,2,0,1:T(8,128)}), f32[1,32,128,128]{3,2,0,1:T(8,128)}) %all-gather.2.cloned.1.call-update) | async-done | bytes 2097168 | tf_op jit(solution)/shard_map/all_gather | solution.py:51
  97.4 4.0 %fusion.16 = f32[6,128,2,128]{3,0,1,2:T(8,128)S(1)} fusion(f32[1,32,128,128]{3,2,0,1:T(8,128)} %all-gather.2.cloned.1.call-done, f32[32,6]{0,1:T(8,128)S(1)} %copy.32, f32[32,2]{0,1:T(2,128)S(1)} %compare_convert_fusion), kind=kOutput, calls=%fused_computation.19 | convolution fusion | flops 75497856 | bytes 2884608 | tf_op jit(solution)/shard_map/kbj,krc->brjc/dot_general | solution.py:63
  101.4 0.3 copy.35
  101.8 2.1 collective-permute-start
  103.9 7.0 %collective-permute-start.1 = (f32[6,128,20]{1,2,0:T(8,128)S(1)}, f32[6,128,20]{1,2,0:T(8,128)S(1)}, u32[]{:S(2)}, u32[]{:S(2)}) collective-permute-start(f32[6,128,20]{1,2,0:T(8,128)S(1)} %get-tuple-element.14), channel_id=1, source_target_pairs={{1,0},{2,1},{3,2},{4,3},{5,4},{6,5},{7,6},{8,7},{9,8},{10,9},{11,1... | collective-permute-start | bytes 184328 | tf_op jit(solution)/shard_map/ppermute | solution.py:17
  111.0 1.5 fusion.21
  112.5 0.1 rev.6
  112.5 0.4 collective-permute-done.1
  112.9 0.1 fusion.53
  113.0 1.5 fusion.35
  114.6 0.3 copy.37
  114.9 3.7 %collective-permute-start.2 = (f32[6,20,256]{2,1,0:T(8,128)S(1)}, f32[6,20,256]{2,1,0:T(8,128)S(1)}, u32[]{:S(2)}, u32[]{:S(2)}) collective-permute-start(f32[6,20,256]{2,1,0:T(8,128)S(1)} %get-tuple-element.9), channel_id=1, source_target_pairs={{0,32},{32,64},{64,96},{96,128},{128,160},{160,192},{192,224},{224... | collective-permute-start | bytes 368648 | tf_op jit(solution)/shard_map/ppermute | solution.py:16
  118.6 2.3 collective-permute-start.3
  120.9 1.5 fusion.20
  122.4 3.2 %collective-permute-done.3 = f32[6,20,256]{2,1,0:T(8,128)S(1)} collective-permute-done((f32[6,20,256]{2,1,0:T(8,128)S(1)}, f32[6,20,256]{2,1,0:T(8,128)S(1)}, u32[]{:S(2)}, u32[]{:S(2)}) %collective-permute-start.3) | collective-permute-done | bytes 122912 | tf_op jit(solution)/shard_map/ppermute | solution.py:17
  125.6 1.5 fusion.19
  127.2 4.4 %collective-permute-start.4 = (f32[6,20,256]{2,1,0:T(8,128)S(1)}, f32[6,20,256]{2,1,0:T(8,128)S(1)}, u32[]{:S(2)}, u32[]{:S(2)}) collective-permute-start(f32[6,20,256]{2,1,0:T(8,128)S(1)} %get-tuple-element.7), channel_id=1, source_target_pairs={{0,32},{32,64},{64,96},{96,128},{128,160},{160,192},{192,224},{224... | collective-permute-start | bytes 368648 | tf_op jit(solution)/shard_map/ppermute | solution.py:16
  131.6 2.1 collective-permute-start.5
  133.7 1.5 fusion.22
  135.2 4.6 %collective-permute-done.5 = f32[6,20,256]{2,1,0:T(8,128)S(1)} collective-permute-done((f32[6,20,256]{2,1,0:T(8,128)S(1)}, f32[6,20,256]{2,1,0:T(8,128)S(1)}, u32[]{:S(2)}, u32[]{:S(2)}) %collective-permute-start.5) | collective-permute-done | bytes 122912 | tf_op jit(solution)/shard_map/ppermute | solution.py:17
  139.9 1.5 fusion.44
  141.4 0.2 fusion.74
  141.6 1.9 collective-permute-start.6
  143.5 7.3 %collective-permute-start.7 = (f32[6,128,20]{2,1,0:T(8,128)S(1)}, f32[6,128,20]{2,1,0:T(8,128)S(1)}, u32[]{:S(2)}, u32[]{:S(2)}) collective-permute-start(f32[6,128,20]{2,1,0:T(8,128)S(1)} %get-tuple-element.6), channel_id=1, source_target_pairs={{1,0},{2,1},{3,2},{4,3},{5,4},{6,5},{7,6},{8,7},{9,8},{10,9},{11,1... | collective-permute-start | bytes 184328 | tf_op jit(solution)/shard_map/ppermute | solution.py:17
  150.8 1.5 fusion.23
  152.3 2.1 collective-permute-done.6
  154.4 1.7 collective-permute-done.7
  156.0 0.6 fusion.51
  156.6 1.6 fusion.14
  158.2 2.5 convolution_bitcast_fusion
  160.7 2.5 copy.45
  163.3 0.0 reduce-scatter.2.cloned.1.call-update
  164.1 0.6 fusion.70
  165.4 4.6 %fusion.30 = f32[32,6]{0,1:T(8,128)S(1)} fusion(f32[1,32,128,128]{3,2,0,1:T(8,128)S(1)} %copy-done, f32[6,128,2,128]{3,1,2,0:T(8,128)S(1)} %fusion.14, f32[32,2]{0,1:T(2,128)S(1)} %compare_convert_fusion), kind=kOutput, calls=%fused_computation.28 | convolution fusion | flops 75498048 | bytes 2884608 | tf_op jit(solution)/shard_map/krc,brjc->kbj/dot_general | solution.py:81
  170.1 0.1 copy.47
  170.2 134.2 %all-reduce.1 = f32[32,6]{1,0:T(8,128)S(1)} all-reduce(f32[32,6]{1,0:T(8,128)S(1)} %copy.47), channel_id=3, replica_groups=mesh['ty'=16,'tx'=32] {'tx'}, use_global_device_ids=true, to_apply=%region_4.0.clone | all-reduce | flops 192 | bytes 1536
  304.4 2.1 fusion.60
  307.2 1.2 maximum_bitcast_fusion
  (26 shorter events, 0.1 us)
Async XLA Ops:
  7.2 90.2 %all-gather.2.cloned.1.call-start = ((), (), s32[]{:S(2)}) async-start(), calls=%async_computation.1 | async-start | bytes 2162688 | tf_op jit(solution)/shard_map/all_gather | solution.py:51
  7.9 296.5 %reduce-scatter.2.cloned.1.call-start = ((), (), s32[]{:S(2)}) async-start(), calls=%async_computation.2 | async-start | bytes 2162688 | tf_op jit(solution)/shard_map/reduce_scatter | solution.py:84
  101.4 11.0 %copy-start.5 = (f32[6,41]{1,0:T(8,128)S(1)}, f32[6,41]{1,0:T(8,128)}, u32[]{:S(2)}) copy-start(f32[6,41]{1,0:T(8,128)} %param.14) | copy-start | bytes 2956
  101.8 10.8 %collective-permute-start = (f32[6,128,20]{1,2,0:T(8,128)S(1)}, f32[6,128,20]{1,2,0:T(8,128)S(1)}, u32[]{:S(2)}, u32[]{:S(2)}) collective-permute-start(f32[6,128,20]{1,2,0:T(8,128)S(1)} %get-tuple-element.13), channel_id=1, source_target_pairs={{0,1},{1,2},{2,3},{3,4},{4,5},{5,6},{6,7},{7,8},{8,9},{9,10},{10,1... | collective-permute-start | bytes 184328 | tf_op jit(solution)/shard_map/ppermute | solution.py:16
  103.9 9.0 %collective-permute-start.1 = (f32[6,128,20]{1,2,0:T(8,128)S(1)}, f32[6,128,20]{1,2,0:T(8,128)S(1)}, u32[]{:S(2)}, u32[]{:S(2)}) collective-permute-start(f32[6,128,20]{1,2,0:T(8,128)S(1)} %get-tuple-element.14), channel_id=1, source_target_pairs={{1,0},{2,1},{3,2},{4,3},{5,4},{6,5},{7,6},{8,7},{9,8},{10,9},{11,1... | collective-permute-start | bytes 184328 | tf_op jit(solution)/shard_map/ppermute | solution.py:17
  114.5 11.1 %copy-start.2 = (f32[6,128,256]{2,1,0:T(8,128)S(1)}, f32[6,128,256]{2,1,0:T(8,128)}, u32[]{:S(2)}) copy-start(f32[6,128,256]{2,1,0:T(8,128)} %param.9) | copy-start | bytes 2359300
  114.6 11.1 %copy-start.3 = (f32[6,128,256]{2,1,0:T(8,128)S(1)}, f32[6,128,256]{2,1,0:T(8,128)}, u32[]{:S(2)}) copy-start(f32[6,128,256]{2,1,0:T(8,128)} %param.8) | copy-start | bytes 2359300
  114.9 7.5 %collective-permute-start.2 = (f32[6,20,256]{2,1,0:T(8,128)S(1)}, f32[6,20,256]{2,1,0:T(8,128)S(1)}, u32[]{:S(2)}, u32[]{:S(2)}) collective-permute-start(f32[6,20,256]{2,1,0:T(8,128)S(1)} %get-tuple-element.9), channel_id=1, source_target_pairs={{0,32},{32,64},{64,96},{96,128},{128,160},{160,192},{192,224},{224... | collective-permute-start | bytes 368648 | tf_op jit(solution)/shard_map/ppermute | solution.py:16
  118.6 7.0 %collective-permute-start.3 = (f32[6,20,256]{2,1,0:T(8,128)S(1)}, f32[6,20,256]{2,1,0:T(8,128)S(1)}, u32[]{:S(2)}, u32[]{:S(2)}) collective-permute-start(f32[6,20,256]{2,1,0:T(8,128)S(1)} %get-tuple-element.10), channel_id=1, source_target_pairs={{32,0},{64,32},{96,64},{128,96},{160,128},{192,160},{224,192},{256... | collective-permute-start | bytes 368648 | tf_op jit(solution)/shard_map/ppermute | solution.py:17
  127.2 14.4 %copy-start.1 = (f32[6,128,256]{2,1,0:T(8,128)}, f32[6,128,256]{2,1,0:T(8,128)S(1)}, u32[]{:S(2)}) copy-start(f32[6,128,256]{2,1,0:T(8,128)S(1)} %fusion.19) | copy-start | bytes 2359300
  127.2 8.0 %collective-permute-start.4 = (f32[6,20,256]{2,1,0:T(8,128)S(1)}, f32[6,20,256]{2,1,0:T(8,128)S(1)}, u32[]{:S(2)}, u32[]{:S(2)}) collective-permute-start(f32[6,20,256]{2,1,0:T(8,128)S(1)} %get-tuple-element.7), channel_id=1, source_target_pairs={{0,32},{32,64},{64,96},{96,128},{128,160},{160,192},{192,224},{224... | collective-permute-start | bytes 368648 | tf_op jit(solution)/shard_map/ppermute | solution.py:16
  131.6 8.2 %collective-permute-start.5 = (f32[6,20,256]{2,1,0:T(8,128)S(1)}, f32[6,20,256]{2,1,0:T(8,128)S(1)}, u32[]{:S(2)}, u32[]{:S(2)}) collective-permute-start(f32[6,20,256]{2,1,0:T(8,128)S(1)} %get-tuple-element.8), channel_id=1, source_target_pairs={{32,0},{64,32},{96,64},{128,96},{160,128},{192,160},{224,192},{256... | collective-permute-start | bytes 368648 | tf_op jit(solution)/shard_map/ppermute | solution.py:17
  135.2 15.6 %copy-start.6 = (f32[6,41]{1,0:T(8,128)S(1)}, f32[6,41]{1,0:T(8,128)}, u32[]{:S(2)}) copy-start(f32[6,41]{1,0:T(8,128)} %param.15) | copy-start | bytes 2956
  141.6 12.8 %collective-permute-start.6 = (f32[6,128,20]{2,1,0:T(8,128)S(1)}, f32[6,128,20]{2,1,0:T(8,128)S(1)}, u32[]{:S(2)}, u32[]{:S(2)}) collective-permute-start(f32[6,128,20]{2,1,0:T(8,128)S(1)} %get-tuple-element.5), channel_id=1, source_target_pairs={{0,1},{1,2},{2,3},{3,4},{4,5},{5,6},{6,7},{7,8},{8,9},{9,10},{10,1... | collective-permute-start | bytes 184328 | tf_op jit(solution)/shard_map/ppermute | solution.py:16
  143.5 12.5 %collective-permute-start.7 = (f32[6,128,20]{2,1,0:T(8,128)S(1)}, f32[6,128,20]{2,1,0:T(8,128)S(1)}, u32[]{:S(2)}, u32[]{:S(2)}) collective-permute-start(f32[6,128,20]{2,1,0:T(8,128)S(1)} %get-tuple-element.6), channel_id=1, source_target_pairs={{1,0},{2,1},{3,2},{4,3},{5,4},{6,5},{7,6},{8,7},{9,8},{10,9},{11,1... | collective-permute-start | bytes 184328 | tf_op jit(solution)/shard_map/ppermute | solution.py:17
  163.3 0.8 copy-start.7
  163.3 2.1 copy-start
  163.3 141.1 %copy-start.4 = (f32[1,1,128,128]{3,2,1,0:T(8,128)S(1)}, f32[1,1,128,128]{3,2,1,0:T(8,128)}, u32[]{:S(2)}) copy-start(f32[1,1,128,128]{3,2,1,0:T(8,128)} %param.11) | copy-start | bytes 196612
Sparse Core Ops, SparseCore 0:
  11.3 86.0 all-gather.1
  163.4 126.2 reduce-scatter.1
where the time goes:
time: 316 us; the launch traced here: 315 us
  blocking collectives  188 us (59%)
  waiting for transfers between devices  45.2 us (14%)
  starting transfers between devices  30.9 us (10%)
  matrix products  23.3 us (7%)
  between operations  17.1 us (5%)
  local copies, waits for them, and re-layouts  6.49 us (2%)
  other arithmetic  4.64 us (1%)
    unnamed x2, blocking collectives  148 us
    all_gather x1, blocking collectives, body(): lax.all_gather(sed, 'tx', axis=1, tiled=True)  39.6 us
    all_gather x1, waiting for transfers between devices, body(): lax.all_gather(morph, 'tx', axis=1, tiled=True)  32.4 us
    ppermute x4, starting transfers between devices, with_halo(): after = lax.ppermute(leading, axis, down)  18.7 us
    ppermute x4, starting transfers between devices, with_halo(): before = lax.ppermute(last, axis, up)  12.1 us
    ppermute x4, waiting for transfers between devices, with_halo(): after = lax.ppermute(leading, axis, down)  9.93 us
  transfers between devices with their start and end apart: 10, of which 6 were waited for; matrix products, arithmetic and copies ran while one was open for 5% of the time, Pallas kernels for 0%

commit v1 on v0

--- a/solution.py
+++ b/solution.py
@@ -4,6 +4,13 @@
 from jax.sharding import PartitionSpec as P
 
 HIGHEST_PRECISION = lax.Precision.HIGHEST
+
+
+def exchange_gather(block, name, dim):
+    size = lax.axis_size(name)
+    pieces = jnp.stack([block for _ in range(size)])
+    pieces = lax.all_to_all(pieces, name, split_axis=0, concat_axis=0)
+    return jnp.concatenate(pieces, axis=dim)
 
 
 def with_halo(value, sides, width):
@@ -48,7 +55,7 @@
     rim_width = (row_kernel.shape[1] - 1) // 2
     all_sed, all_morph, all_foot = (
         lax.all_gather(sed, "tx", axis=1, tiled=True),
-        lax.all_gather(morph, "tx", axis=1, tiled=True),
+        exchange_gather(morph, "tx", 1),
         lax.all_gather(foot_block, "tx", axis=1, tiled=True),
     )
     all_sed = all_sed[0]

time: 316 us -> 342 us (1.082)
  the two profiles are of different devices: /device:TPU:96 before, /device:TPU:34 now
where the time goes in v1:
time: 342 us; the launch traced here: 341 us
  blocking collectives  227 us (66%)
  starting transfers between devices  49.9 us (15%)
  matrix products  23.8 us (7%)
  between operations  17 us (5%)
  local copies, waits for them, and re-layouts  10.4 us (3%)
  waiting for transfers between devices  7.5 us (2%)
  other arithmetic  5.72 us (2%)
    unnamed x2, blocking collectives  150 us
    all_gather x1, blocking collectives, body(): lax.all_gather(sed, 'tx', axis=1, tiled=True)  77.3 us
    ppermute x4, starting transfers between devices, with_halo(): after = lax.ppermute(leading, axis, down)  30.7 us
    ppermute x4, starting transfers between devices, with_halo(): before = lax.ppermute(last, axis, up)  10.2 us
    all_to_all x1, starting transfers between devices, exchange_gather(): pieces = lax.all_to_all(pieces, name, split_axis=0, concat_axis=0)  9.06 us
  transfers between devices with their start and end apart: 10, of which 6 were waited for; matrix products, arithmetic and copies ran while one was open for 4% of the time, Pallas kernels for 0%

profile of v1, /device:TPU:34, one launch (start us, length us, event | category | flops | bytes accessed | tf_op | source)
XLA Modules:
  0.0 341.4 jit_solution(16911249605065898569)
XLA Ops:
  7.2 2.4 stack.14
  9.6 9.1 %all-to-all-start = ((f32[32,1,1,128,128]{4,3,2,1,0:T(8,128)}), f32[32,1,1,128,128]{4,3,2,1,0:T(8,128)S(1)}, u32[]{:S(2)}, u32[]{:S(2)}) async-start(f32[32,1,1,128,128]{4,3,2,1,0:T(8,128)} %stack.14), calls=%async_computation | async-start | bytes 4194304 | tf_op jit(solution)/shard_map/all_to_all | solution.py:12
  18.7 0.0 reduce-scatter.2.cloned.1.call-start
  19.4 0.1 rev.7
  19.4 77.3 %all_gather.7 = f32[1,32,6]{2,0,1:T(1,128)S(1)} all-gather(f32[1,1,6]{2,0,1:T(1,128)S(1)} %bitcast.109), channel_id=1, replica_groups=mesh['ty'=16,'tx'=32] {'tx'}, dimensions={1}, use_global_device_ids=true | all-gather | bytes 792 | tf_op jit(solution)/shard_map/all_gather | solution.py:57
  96.8 0.1 copy.30
  96.9 0.6 fusion.78
  97.5 0.7 bitcast_dynamic-update-slice_fusion
  98.2 15.6 %all-reduce = s32[32]{0:T(128)S(1)} all-reduce(s32[32]{0:T(128)S(1)} %bitcast_dynamic-update-slice_fusion), channel_id=1, replica_groups=mesh['ty'=16,'tx'=32] {'tx'}, use_global_device_ids=true, to_apply=%add | all-reduce | flops 32 | bytes 256
  113.7 0.1 compare_convert_fusion
  113.8 2.5 fusion.16
  116.3 1.2 copy.32
  117.5 0.9 fusion.77
  118.4 1.9 collective-permute-start
  120.4 7.3 %collective-permute-start.1 = (f32[6,128,20]{1,2,0:T(8,128)S(1)}, f32[6,128,20]{1,2,0:T(8,128)S(1)}, u32[]{:S(2)}, u32[]{:S(2)}) collective-permute-start(f32[6,128,20]{1,2,0:T(8,128)S(1)} %get-tuple-element.14), channel_id=1, source_target_pairs={{1,0},{2,1},{3,2},{4,3},{5,4},{6,5},{7,6},{8,7},{9,8},{10,9},{11,1... | collective-permute-start | bytes 184328 | tf_op jit(solution)/shard_map/ppermute | solution.py:24
  127.6 1.5 fusion.21
  129.1 0.1 rev.6
  129.2 0.4 collective-permute-done.1
  129.6 1.2 fusion.53
  130.8 2.4 fusion.35
  133.2 1.4 copy.34
  134.7 4.4 %collective-permute-start.2 = (f32[6,20,256]{2,1,0:T(8,128)S(1)}, f32[6,20,256]{2,1,0:T(8,128)S(1)}, u32[]{:S(2)}, u32[]{:S(2)}) collective-permute-start(f32[6,20,256]{2,1,0:T(8,128)S(1)} %get-tuple-element.9), channel_id=1, source_target_pairs={{0,32},{32,64},{64,96},{96,128},{128,160},{160,192},{192,224},{224... | collective-permute-start | bytes 368648 | tf_op jit(solution)/shard_map/ppermute | solution.py:23
  139.1 9.5 %collective-permute-start.3 = (f32[6,20,256]{2,1,0:T(8,128)S(1)}, f32[6,20,256]{2,1,0:T(8,128)S(1)}, u32[]{:S(2)}, u32[]{:S(2)}) collective-permute-start(f32[6,20,256]{2,1,0:T(8,128)S(1)} %get-tuple-element.10), channel_id=1, source_target_pairs={{32,0},{64,32},{96,64},{128,96},{160,128},{192,160},{224,192},{256... | collective-permute-start | bytes 368648 | tf_op jit(solution)/shard_map/ppermute | solution.py:24
  148.6 1.5 fusion.20
  150.1 1.0 collective-permute-done.2
  151.0 1.2 collective-permute-done.3
  152.2 2.7 fusion.19
  155.0 1.9 collective-permute-start.4
  156.9 6.7 %collective-permute-start.5 = (f32[6,20,256]{2,1,0:T(8,128)S(1)}, f32[6,20,256]{2,1,0:T(8,128)S(1)}, u32[]{:S(2)}, u32[]{:S(2)}) collective-permute-start(f32[6,20,256]{2,1,0:T(8,128)S(1)} %get-tuple-element.8), channel_id=1, source_target_pairs={{32,0},{64,32},{96,64},{128,96},{160,128},{192,160},{224,192},{256... | collective-permute-start | bytes 368648 | tf_op jit(solution)/shard_map/ppermute | solution.py:24
  163.6 1.5 fusion.22
  165.1 1.1 collective-permute-done.5
  166.2 1.5 fusion.44
  167.7 0.2 fusion.74
  167.9 1.9 collective-permute-start.6
  169.8 7.3 %collective-permute-start.7 = (f32[6,128,20]{2,1,0:T(8,128)S(1)}, f32[6,128,20]{2,1,0:T(8,128)S(1)}, u32[]{:S(2)}, u32[]{:S(2)}) collective-permute-start(f32[6,128,20]{2,1,0:T(8,128)S(1)} %get-tuple-element.6), channel_id=1, source_target_pairs={{1,0},{2,1},{3,2},{4,3},{5,4},{6,5},{7,6},{8,7},{9,8},{10,9},{11,1... | collective-permute-start | bytes 184328 | tf_op jit(solution)/shard_map/ppermute | solution.py:24
  177.1 1.5 fusion.23
  178.6 2.1 collective-permute-done.6
  180.7 1.7 collective-permute-done.7
  182.4 0.6 fusion.51
  183.0 1.6 fusion.14
  184.5 2.5 convolution_bitcast_fusion
  187.1 2.6 copy.42
  190.3 0.6 fusion.70
  191.6 4.6 %fusion.30 = f32[32,6]{0,1:T(8,128)S(1)} fusion(f32[32,1,1,128,128]{4,3,2,1,0:T(8,128)S(1)} %all-to-all-done, f32[6,128,2,128]{3,1,2,0:T(8,128)S(1)} %fusion.14, f32[32,2]{0,1:T(2,128)S(1)} %compare_convert_fusion), kind=kOutput, calls=%fused_computation.28 | convolution fusion | flops 75498048 | bytes 2884608 | tf_op jit(solution)/shard_map/krc,brjc->kbj/dot_general | solution.py:88
  196.3 0.1 copy.44
  196.4 134.2 %all-reduce.1 = f32[32,6]{1,0:T(8,128)S(1)} all-reduce(f32[32,6]{1,0:T(8,128)S(1)} %copy.44), channel_id=3, replica_groups=mesh['ty'=16,'tx'=32] {'tx'}, use_global_device_ids=true, to_apply=%region_4.0.clone | all-reduce | flops 192 | bytes 1536
  330.6 2.1 fusion.60
  333.4 1.1 maximum_bitcast_fusion
  (24 shorter events, 0.1 us)
Async XLA Ops:
  9.6 9.8 %copy-start.4 = (f32[6,41]{1,0:T(8,128)S(1)}, f32[6,41]{1,0:T(8,128)}, u32[]{:S(2)}) copy-start(f32[6,41]{1,0:T(8,128)} %param.15) | copy-start | bytes 2956
  9.6 9.9 %copy-start.5 = (f32[1,1,6]{2,1,0:T(1,128)S(1)}, f32[1,1,6]{2,1,0:T(1,128)}, u32[]{:S(2)}) copy-start(f32[1,1,6]{2,1,0:T(1,128)} %param.10) | copy-start | bytes 76
  9.6 87.3 %copy-start.6 = (u32[512]{0:T(512)S(1)}, u32[512]{0:T(512)}, u32[]{:S(2)}) copy-start(u32[512]{0:T(512)} %constant.16) | copy-start | bytes 6148
  9.6 104.2 %all-to-all-start = ((f32[32,1,1,128,128]{4,3,2,1,0:T(8,128)}), f32[32,1,1,128,128]{4,3,2,1,0:T(8,128)S(1)}, u32[]{:S(2)}, u32[]{:S(2)}) async-start(f32[32,1,1,128,128]{4,3,2,1,0:T(8,128)} %stack.14), calls=%async_computation | async-start | bytes 4194304 | tf_op jit(solution)/shard_map/all_to_all | solution.py:12
  18.7 312.0 %reduce-scatter.2.cloned.1.call-start = ((), (), s32[]{:S(2)}) async-start(), calls=%async_computation.2 | async-start | bytes 2162688 | tf_op jit(solution)/shard_map/reduce_scatter | solution.py:91
  116.3 12.8 %copy-start.3 = (f32[6,41]{1,0:T(8,128)S(1)}, f32[6,41]{1,0:T(8,128)}, u32[]{:S(2)}) copy-start(f32[6,41]{1,0:T(8,128)} %param.14) | copy-start | bytes 2956
  118.4 10.8 %collective-permute-start = (f32[6,128,20]{1,2,0:T(8,128)S(1)}, f32[6,128,20]{1,2,0:T(8,128)S(1)}, u32[]{:S(2)}, u32[]{:S(2)}) collective-permute-start(f32[6,128,20]{1,2,0:T(8,128)S(1)} %get-tuple-element.13), channel_id=1, source_target_pairs={{0,1},{1,2},{2,3},{3,4},{4,5},{5,6},{6,7},{7,8},{8,9},{9,10},{10,1... | collective-permute-start | bytes 184328 | tf_op jit(solution)/shard_map/ppermute | solution.py:23
  120.4 9.2 %collective-permute-start.1 = (f32[6,128,20]{1,2,0:T(8,128)S(1)}, f32[6,128,20]{1,2,0:T(8,128)S(1)}, u32[]{:S(2)}, u32[]{:S(2)}) collective-permute-start(f32[6,128,20]{1,2,0:T(8,128)S(1)} %get-tuple-element.14), channel_id=1, source_target_pairs={{1,0},{2,1},{3,2},{4,3},{5,4},{6,5},{7,6},{8,7},{9,8},{10,9},{11,1... | collective-permute-start | bytes 184328 | tf_op jit(solution)/shard_map/ppermute | solution.py:24
  134.6 17.6 %copy-start.1 = (f32[6,128,256]{2,1,0:T(8,128)S(1)}, f32[6,128,256]{2,1,0:T(8,128)}, u32[]{:S(2)}) copy-start(f32[6,128,256]{2,1,0:T(8,128)} %param.9) | copy-start | bytes 2359300
  134.7 16.4 %collective-permute-start.2 = (f32[6,20,256]{2,1,0:T(8,128)S(1)}, f32[6,20,256]{2,1,0:T(8,128)S(1)}, u32[]{:S(2)}, u32[]{:S(2)}) collective-permute-start(f32[6,20,256]{2,1,0:T(8,128)S(1)} %get-tuple-element.9), channel_id=1, source_target_pairs={{0,32},{32,64},{64,96},{96,128},{128,160},{160,192},{192,224},{224... | collective-permute-start | bytes 368648 | tf_op jit(solution)/shard_map/ppermute | solution.py:23
  139.1 13.1 %collective-permute-start.3 = (f32[6,20,256]{2,1,0:T(8,128)S(1)}, f32[6,20,256]{2,1,0:T(8,128)S(1)}, u32[]{:S(2)}, u32[]{:S(2)}) collective-permute-start(f32[6,20,256]{2,1,0:T(8,128)S(1)} %get-tuple-element.10), channel_id=1, source_target_pairs={{32,0},{64,32},{96,64},{128,96},{160,128},{192,160},{224,192},{256... | collective-permute-start | bytes 368648 | tf_op jit(solution)/shard_map/ppermute | solution.py:24
  154.9 13.0 %copy-start = (f32[6,128,256]{2,1,0:T(8,128)}, f32[6,128,256]{2,1,0:T(8,128)S(1)}, u32[]{:S(2)}) copy-start(f32[6,128,256]{2,1,0:T(8,128)S(1)} %fusion.19) | copy-start | bytes 2359300
  155.0 10.1 %collective-permute-start.4 = (f32[6,20,256]{2,1,0:T(8,128)S(1)}, f32[6,20,256]{2,1,0:T(8,128)S(1)}, u32[]{:S(2)}, u32[]{:S(2)}) collective-permute-start(f32[6,20,256]{2,1,0:T(8,128)S(1)} %get-tuple-element.7), channel_id=1, source_target_pairs={{0,32},{32,64},{64,96},{96,128},{128,160},{160,192},{192,224},{224... | collective-permute-start | bytes 368648 | tf_op jit(solution)/shard_map/ppermute | solution.py:23
  156.9 9.3 %collective-permute-start.5 = (f32[6,20,256]{2,1,0:T(8,128)S(1)}, f32[6,20,256]{2,1,0:T(8,128)S(1)}, u32[]{:S(2)}, u32[]{:S(2)}) collective-permute-start(f32[6,20,256]{2,1,0:T(8,128)S(1)} %get-tuple-element.8), channel_id=1, source_target_pairs={{32,0},{64,32},{96,64},{128,96},{160,128},{192,160},{224,192},{256... | collective-permute-start | bytes 368648 | tf_op jit(solution)/shard_map/ppermute | solution.py:24
  167.9 12.8 %collective-permute-start.6 = (f32[6,128,20]{2,1,0:T(8,128)S(1)}, f32[6,128,20]{2,1,0:T(8,128)S(1)}, u32[]{:S(2)}, u32[]{:S(2)}) collective-permute-start(f32[6,128,20]{2,1,0:T(8,128)S(1)} %get-tuple-element.5), channel_id=1, source_target_pairs={{0,1},{1,2},{2,3},{3,4},{4,5},{5,6},{6,7},{7,8},{8,9},{9,10},{10,1... | collective-permute-start | bytes 184328 | tf_op jit(solution)/shard_map/ppermute | solution.py:23
  169.8 12.5 %collective-permute-start.7 = (f32[6,128,20]{2,1,0:T(8,128)S(1)}, f32[6,128,20]{2,1,0:T(8,128)S(1)}, u32[]{:S(2)}, u32[]{:S(2)}) collective-permute-start(f32[6,128,20]{2,1,0:T(8,128)S(1)} %get-tuple-element.6), channel_id=1, source_target_pairs={{1,0},{2,1},{3,2},{4,3},{5,4},{6,5},{7,6},{8,7},{9,8},{10,9},{11,1... | collective-permute-start | bytes 184328 | tf_op jit(solution)/shard_map/ppermute | solution.py:24
  189.6 141.0 %copy-start.2 = (f32[1,1,128,128]{3,2,1,0:T(8,128)S(1)}, f32[1,1,128,128]{3,2,1,0:T(8,128)}, u32[]{:S(2)}) copy-start(f32[1,1,128,128]{3,2,1,0:T(8,128)} %param.11) | copy-start | bytes 196612
Sparse Core Ops, SparseCore 0:
  189.8 126.1 reduce-scatter.1
